TPU v7x, 32 devices: a whole 2x2x4 slice. The times are simulated.
32 devices in a mesh: wide: 8 (over z, x), narrow: 4 (over y, core).
Axes of the slice: x: 2, y: 2, z: 4, core: 2. Of those that a mesh axis runs over, the one named last changes fastest.
Arguments:
- embeddings: bfloat16 [16384, 1024], P(('wide', 'narrow')), may hold values from -32 to 32
- valid: int32 [16384], P(('wide', 'narrow')), may hold values from 0 to 1, as said below
Outputs:
- whitened: bfloat16 [16384, 1024], P(('wide', 'narrow'))
Inputs may be any that keep to these rules, and one draw needn't show every extreme that they name: The first row of every aligned block of 16 rows has valid = 1.
All inputs are finite; a program needn't handle non-finite values.
Results may differ from a plain program's by a relative error of at most 0.001.
Values sent between devices are 32-bit elements; how exact they have to be, the bound alone decides.
No kernel may reach another device: no remote copies, remote signals or barrier semaphores. Data moves between devices by JAX's collectives and lax.ppermute only.
A program may use at most 64 MiB of HBM per device.

v0:
```python
import jax
import jax.numpy as jnp
from jax import lax
from jax.sharding import PartitionSpec as P


def shifted_scatter(gram, count_local, sums_local, center):
    return (
        gram
        - sums_local[:, None] * center[None, :]
        - center[:, None] * sums_local[None, :]
        + count_local * center[:, None] * center[None, :]
    )


def narrow_rows(term):
    return lax.psum_scatter(term, "narrow", scatter_dimension=0, tiled=True)


def on_device(embeddings, valid):
    width = embeddings.shape[1]
    narrow_count = lax.axis_size("narrow")
    row_span = width // narrow_count
    offset = lax.axis_index("narrow") * row_span
    mask_half = valid.astype(jnp.bfloat16)
    count_local = jnp.sum(valid.astype(jnp.float32))
    masked = embeddings * mask_half[:, None]
    gram = lax.dot_general(
        masked, embeddings, (((0,), (0,)), ((), ())), preferred_element_type=jnp.float32
    )
    sums_local = jnp.dot(mask_half[None, :], embeddings, preferred_element_type=jnp.float32)[0]
    count, sums = lax.psum((count_local, sums_local), ("wide", "narrow"))
    term = shifted_scatter(gram, count_local, sums_local, sums / count)
    level_rows = narrow_rows(term)
    own_rows = lax.psum(level_rows, "wide")
    center = sums / count
    cov_rows = own_rows / count
    ident_rows = (
        lax.broadcasted_iota(jnp.int32, (row_span, width), 0) + offset
        == lax.broadcasted_iota(jnp.int32, (row_span, width), 1)
    ).astype(jnp.float32)
    diag_block = lax.dynamic_slice_in_dim(cov_rows, offset, row_span, 1)
    trace_part = jnp.sum(jnp.diagonal(diag_block))
    square_part = jnp.sum(cov_rows * cov_rows)
    trace_cov, square_sum = lax.psum((trace_part, square_part), "narrow")
    ridge_add = 0.05 * trace_cov / width + 1e-06
    norm_frob = jnp.sqrt(square_sum + 2.0 * ridge_add * trace_cov + width * ridge_add * ridge_add)
    base_rows = (cov_rows + ridge_add * ident_rows) / norm_frob
    root_rows = (3.0 * ident_rows - base_rows) / 2.0
    root_full = lax.all_gather(root_rows, "narrow", axis=0, tiled=True)
    first = jnp.dot(
        base_rows, root_full, precision=lax.Precision.HIGHEST, preferred_element_type=jnp.float32
    )
    second = jnp.dot(
        first, root_full, precision=lax.Precision.HIGHEST, preferred_element_type=jnp.float32
    )
    factor = (3.0 * ident_rows - second) / 2.0
    root_rows = jnp.dot(
        factor, root_full, precision=lax.Precision.HIGHEST, preferred_element_type=jnp.float32
    )
    centered_x = embeddings.astype(jnp.float32) - center
    product = jnp.dot(
        centered_x,
        lax.all_gather(root_rows, "narrow", axis=0, tiled=True),
        precision=lax.Precision.HIGHEST,
        preferred_element_type=jnp.float32,
    )
    return (product / jnp.sqrt(norm_frob)).astype(jnp.bfloat16)


def solution(mesh):
    in_specs = (P(("wide", "narrow"), None), P(("wide", "narrow")))
    out_specs = P(("wide", "narrow"), None)
    return jax.shard_map(
        on_device, mesh=mesh, in_specs=in_specs, out_specs=out_specs, check_vma=False
    )
```

profile of v0, /device:TPU:0, one launch (start us, length us, event | category | flops | bytes accessed | tf_op | source)
XLA Modules:
  0.0 300.6 jit_solution(4755402428084836865)
XLA Ops:
  6.5 0.0 reduce-scatter.2.cloned.1.call-start
  6.5 0.7 convert_element_type.14
  7.2 1.3 convert_reduce_fusion
  8.5 1.5 fusion.11
  10.0 42.1 %all-reduce = (f32[1024]{0:T(1024)S(1)}, f32[]{:T(128)}) all-reduce(f32[1024]{0:T(1024)S(1)} %bitcast.12, f32[]{:T(128)} %convert_reduce_fusion), channel_id=1, replica_groups=mesh['wide'=8,'narrow'=4] {'wide','narrow'}, use_global_device_ids=true, to_apply=%region_0.0 | all-reduce | flops 1025 | bytes 8200 | tf_op jit(solution)/shard_map/psum | solution.py:32
  52.1 1.3 broadcast_multiply_fusion
  53.4 5.3 %multiply_add_fusion = f32[1024,1024]{1,0:T(8,128)} fusion(bf16[512,1024]{1,0:T(8,128)(2,1)} %param.2, f32[1024]{0:T(1024)S(1)} %get-tuple-element.11, f32[1024]{0:T(1024)S(1)} %bitcast.13, f32[1024]{0:T(1024)S(1)} %get-tuple-element.12, bf16[512]{0:T(512)(128)(2,1)S(1)} %convert_element_type.14), kind=kOutput, calls=%fused_computation.1 | convolution fusion | flops 1080557568 | bytes 5256192 | tf_op jit(solution)/shard_map/dot_general | solution.py:28
  58.7 0.0 reduce-scatter.2.cloned.1.call-update
  58.7 0.0 all-reduce.4.cloned.1.call-start
  58.8 44.7 %reduce-scatter.2.cloned.1.call-done = f32[256,1024]{1,0:T(8,128)} async-done(((f32[1024,1024]{1,0:T(8,128)}), f32[256,1024]{1,0:T(8,128)}) %reduce-scatter.2.cloned.1.call-update) | async-done | bytes 1048592 | tf_op jit(solution)/shard_map/reduce_scatter | solution.py:17
  103.5 0.0 all-reduce.4.cloned.1.call-update
  103.5 0.0 all-gather.3.cloned.1.call-start
  103.6 81.6 %all-reduce.4.cloned.1.call-done = f32[256,1024]{1,0:T(8,128)} async-done(((f32[256,1024]{1,0:T(8,128)}), f32[256,1024]{1,0:T(8,128)}) %all-reduce.4.cloned.1.call-update) | async-done | bytes 1048592 | tf_op jit(solution)/shard_map/psum | solution.py:35
  185.2 2.7 multiply_reduce_fusion
  188.0 2.3 gather_fusion
  190.4 0.7 reduce_sum.28
  191.0 7.2 %all-reduce.1 = (f32[]{:T(128)}, f32[]{:T(128)}) all-reduce(f32[]{:T(128)} %get-tuple-element.9, f32[]{:T(128)} %reduce_sum.28), channel_id=1, replica_groups=mesh['wide'=8,'narrow'=4] {'narrow'}, use_global_device_ids=true, to_apply=%region_8.9 | all-reduce | flops 2 | bytes 16 | tf_op jit(solution)/shard_map/psum | solution.py:45
  200.3 1.3 fusion.7
  201.6 0.0 all-gather.3.cloned.1.call-update
  201.6 0.2 all-gather.5.cloned.1.call-start
  201.8 33.4 %all-gather.3.cloned.1.call-done = f32[1024,1024]{1,0:T(8,128)} async-done(((f32[256,1024]{1,0:T(8,128)}), f32[1024,1024]{1,0:T(8,128)}) %all-gather.3.cloned.1.call-update) | async-done | bytes 4194320 | tf_op jit(solution)/shard_map/all_gather | solution.py:50
  235.2 0.0 copy-start
  235.2 6.1 %fusion.10 = f32[256,1024]{1,0:T(8,128)S(1)} fusion(f32[1024,1024]{1,0:T(8,128)} %all-gather.3.cloned.1.call-done, f32[256,1024]{1,0:T(8,128)S(1)} %get-tuple-element.10, f32[]{:T(128)S(6)} %sqrt.6, f32[]{:T(128)S(6)} %add.45, s32[256]{0:T(256)S(1)} %iota_add_fusion), kind=kOutput, calls=%fused_computation.23 | convolution fusion | flops 3222274048 | bytes 6292488 | tf_op jit(solution)/shard_map/dot_general | solution.py:51
  241.4 0.0 copy-done
  241.4 3.7 %fusion.4 = f32[256,1024]{1,0:T(8,128)S(1)} fusion(f32[256,1024]{1,0:T(8,128)S(1)} %fusion.10, f32[1024,1024]{1,0:T(8,128)S(1)} %copy-done, s32[256]{0:T(256)S(1)} %iota_add_fusion), kind=kOutput, calls=%fused_computation.9 | convolution fusion | flops 3222274048 | bytes 6292480 | tf_op jit(solution)/shard_map/dot_general | solution.py:54
  245.1 0.0 copy-start.1
  245.2 4.7 %fusion.12 = f32[256,1024]{1,0:T(8,128)} fusion(f32[256,1024]{1,0:T(8,128)S(1)} %fusion.4, f32[1024,1024]{1,0:T(8,128)S(1)} %copy-done), kind=kOutput, calls=%fused_computation.25 | convolution fusion | flops 3221225472 | bytes 6291456 | tf_op jit(solution)/shard_map/dot_general | solution.py:58
  249.8 0.0 all-gather.5.cloned.1.call-update
  249.9 34.6 %all-gather.5.cloned.1.call-done = f32[1024,1024]{1,0:T(8,128)} async-done(((f32[256,1024]{1,0:T(8,128)}), f32[1024,1024]{1,0:T(8,128)}) %all-gather.5.cloned.1.call-update) | async-done | bytes 4194320 | tf_op jit(solution)/shard_map/all_gather | solution.py:64
  284.5 0.0 copy-done.1
  284.5 9.6 %divide_convert_fusion = bf16[512,1024]{1,0:T(8,128)(2,1)} fusion(f32[1024,1024]{1,0:T(8,128)} %all-gather.5.cloned.1.call-done, bf16[512,1024]{1,0:T(8,128)(2,1)S(1)} %copy-done.1, f32[]{:T(128)S(6)} %sqrt.7, f32[1024]{0:T(1024)S(1)} %get-tuple-element.12), kind=kOutput, calls=%fused_computation.2 | convolution fusion | flops 6444548096 | bytes 6295556 | tf_op jit(solution)/shard_map/dot_general | solution.py:62
  (4 shorter events, 0.0 us)
Async XLA Ops:
  6.5 97.0 %reduce-scatter.2.cloned.1.call-start = ((), (), s32[]{:S(2)}) async-start(), calls=%async_computation.1 | async-start | bytes 5242880 | tf_op jit(solution)/shard_map/reduce_scatter | solution.py:17
  58.7 126.5 %all-reduce.4.cloned.1.call-start = ((), (), s32[]{:S(2)}) async-start(), calls=%async_computation.2 | async-start | bytes 2097152 | tf_op jit(solution)/shard_map/psum | solution.py:35
  103.5 131.7 %all-gather.3.cloned.1.call-start = ((), (), s32[]{:S(2)}) async-start(), calls=%async_computation.3 | async-start | bytes 5242880 | tf_op jit(solution)/shard_map/all_gather | solution.py:50
  201.6 82.9 %all-gather.5.cloned.1.call-start = ((), (), s32[]{:S(2)}) async-start(), calls=%async_computation.4 | async-start | bytes 5242880 | tf_op jit(solution)/shard_map/all_gather | solution.py:64
  235.2 6.1 %copy-start = (f32[1024,1024]{1,0:T(8,128)S(1)}, f32[1024,1024]{1,0:T(8,128)}, u32[]{:S(2)}) copy-start(f32[1024,1024]{1,0:T(8,128)} %all-gather.3.cloned.1.call-done) | copy-start | bytes 12582916
  245.1 39.3 %copy-start.1 = (bf16[512,1024]{1,0:T(8,128)(2,1)S(1)}, bf16[512,1024]{1,0:T(8,128)(2,1)}, u32[]{:S(2)}) copy-start(bf16[512,1024]{1,0:T(8,128)(2,1)} %param.2) | copy-start | bytes 3145732
Sparse Core Ops, SparseCore 0:
  58.9 44.6 reduce-scatter.1
  107.0 78.1 all-reduce.3
  201.7 33.4 all-gather.2
  250.0 34.4 all-gather.4
where the time goes:
time: 301 us
  waiting for transfers between devices  194 us (64%)
  blocking collectives  49.3 us (16%)
  matrix products  30.9 us (10%)
  between operations  15.3 us (5%)
  other arithmetic  7.97 us (3%)
    psum x1, waiting for transfers between devices, on_device(): own_rows = lax.psum(level_rows, 'wide')  81.6 us
    reduce_scatter x1, waiting for transfers between devices, narrow_rows(): return lax.psum_scatter(term, 'narrow', scatter_dimension=0, tiled=True)  44.7 us
    psum x1, blocking collectives, on_device(): count, sums = lax.psum((count_local, sums_local), ('wide', 'narrow'))  42.1 us
    all_gather x1, waiting for transfers between devices, on_device(): lax.all_gather(root_rows, 'narrow', axis=0, tiled=True)  34.6 us
    all_gather x1, waiting for transfers between devices, on_device(): root_full = lax.all_gather(root_rows, 'narrow', axis=0, tiled=True)  33.4 us
    dot_general x1, matrix products, on_device(): jnp.dot(centered_x, lax.all_gather(root_rows, 'narrow', axis=0, tiled=Tru...  9.62 us
    psum x1, blocking collectives, on_device(): trace_cov, square_sum = lax.psum((trace_part, square_part), 'narrow')  7.19 us
    dot_general x1, matrix products, on_device(): jnp.dot(base_rows, root_full, precision=lax.Precision.HIGHEST, preferred_...  6.13 us
  transfers between devices with their start and end apart: 4, of which 4 were waited for; matrix products, arithmetic and copies ran while one was open for 0% of the time, Pallas kernels for 0%

commit v1 on v0

--- a/solution.py
+++ b/solution.py
@@ -32,7 +32,7 @@
     count, sums = lax.psum((count_local, sums_local), ("wide", "narrow"))
     term = shifted_scatter(gram, count_local, sums_local, sums / count)
     level_rows = narrow_rows(term)
-    own_rows = lax.psum(level_rows, "wide")
+    own_rows = jnp.sum(lax.all_gather(level_rows, "wide"), axis=0)
     center = sums / count
     cov_rows = own_rows / count
     ident_rows = (

time: 301 us -> 348 us (1.16)
  waiting for transfers between devices: 194 us -> 239 us
    all_gather x0 -> x1, waiting for transfers between devices: none -> 127 us  [on_device(): own_rows = jnp.sum(lax.all_gather(level_rows, 'wide'), axis=0)]
    psum x1 -> x0, waiting for transfers between devices: 81.6 us -> none  [on_device(): own_rows = lax.psum(level_rows, 'wide')]
    reduce_sum x0 -> x1, other arithmetic: none -> 4.42 us  [on_device(): own_rows = jnp.sum(lax.all_gather(level_rows, 'wide'), axis=0)]
where the time goes in v1:
time: 348 us; the launch traced here: 347 us
  waiting for transfers between devices  239 us (69%)
  blocking collectives  48.7 us (14%)
  matrix products  31 us (9%)
  between operations  15.3 us (4%)
  other arithmetic  11.1 us (3%)
    all_gather x1, waiting for transfers between devices, on_device(): own_rows = jnp.sum(lax.all_gather(level_rows, 'wide'), axis=0)  127 us
    reduce_scatter x1, waiting for transfers between devices, narrow_rows(): return lax.psum_scatter(term, 'narrow', scatter_dimension=0, tiled=True)  44.8 us
    psum x1, blocking collectives, on_device(): count, sums = lax.psum((count_local, sums_local), ('wide', 'narrow'))  42.1 us
    all_gather x1, waiting for transfers between devices, on_device(): lax.all_gather(root_rows, 'narrow', axis=0, tiled=True)  34.6 us
    all_gather x1, waiting for transfers between devices, on_device(): root_full = lax.all_gather(root_rows, 'narrow', axis=0, tiled=True)  32.6 us
    dot_general x1, matrix products, on_device(): jnp.dot(centered_x, lax.all_gather(root_rows, 'narrow', axis=0, tiled=Tru...  9.62 us
  transfers between devices with their start and end apart: 4, of which 4 were waited for; matrix products, arithmetic and copies ran while one was open for 0% of the time, Pallas kernels for 0%

profile of v1, /device:TPU:0, one launch (start us, length us, event | category | flops | bytes accessed | tf_op | source)
XLA Modules:
  0.0 347.3 jit_solution(6919717005734200443)
XLA Ops:
  6.5 0.0 reduce-scatter.2.cloned.1.call-start
  6.5 0.7 convert_element_type.14
  7.2 1.3 convert_reduce_fusion
  8.5 1.5 fusion.11
  10.0 42.1 %all-reduce = (f32[1024]{0:T(1024)S(1)}, f32[]{:T(128)}) all-reduce(f32[1024]{0:T(1024)S(1)} %bitcast.14, f32[]{:T(128)} %convert_reduce_fusion), channel_id=1, replica_groups=mesh['wide'=8,'narrow'=4] {'wide','narrow'}, use_global_device_ids=true, to_apply=%region_0.0 | all-reduce | flops 1025 | bytes 8200 | tf_op jit(solution)/shard_map/psum | solution.py:32
  52.1 1.3 broadcast_multiply_fusion
  53.4 5.3 %multiply_add_fusion = f32[1024,1024]{1,0:T(8,128)} fusion(bf16[512,1024]{1,0:T(8,128)(2,1)} %param.2, f32[1024]{0:T(1024)S(1)} %get-tuple-element.11, f32[1024]{0:T(1024)S(1)} %bitcast.15, f32[1024]{0:T(1024)S(1)} %get-tuple-element.12, bf16[512]{0:T(512)(128)(2,1)S(1)} %convert_element_type.14), kind=kOutput, calls=%fused_computation.1 | convolution fusion | flops 1080557568 | bytes 5256192 | tf_op jit(solution)/shard_map/dot_general | solution.py:28
  58.7 0.0 reduce-scatter.2.cloned.1.call-update
  58.7 0.0 all-gather.9.cloned.1.call-start
  58.8 44.8 %reduce-scatter.2.cloned.1.call-done = f32[256,1024]{1,0:T(8,128)} async-done(((f32[1024,1024]{1,0:T(8,128)}), f32[256,1024]{1,0:T(8,128)}) %reduce-scatter.2.cloned.1.call-update) | async-done | bytes 1048592 | tf_op jit(solution)/shard_map/reduce_scatter | solution.py:17
  103.6 0.0 all-gather.9.cloned.1.call-update
  103.6 0.0 all-gather.5.cloned.1.call-start
  103.7 126.5 %all-gather.9.cloned.1.call-done = f32[2048,1024]{1,0:T(8,128)} async-done(((f32[256,1024]{1,0:T(8,128)}), f32[2048,1024]{1,0:T(8,128)}) %all-gather.9.cloned.1.call-update) | async-done | bytes 8388624 | tf_op jit(solution)/shard_map/all_gather | solution.py:35
  230.2 4.4 %reduce_sum.37 = f32[256,1024]{1,0:T(8,128)S(1)} reduce(f32[8,256,1024]{2,1,0:T(8,128)} %bitcast.13, f32[]{:T(128)} %constant.11.clone.1), dimensions={0}, to_apply=%region_4.0 | reduce | flops 1835008 | bytes 9437188 | tf_op jit(solution)/shard_map/reduce_sum | solution.py:35
  234.6 1.5 multiply_reduce_fusion
  236.1 2.3 gather_fusion
  238.5 0.7 reduce_sum.38
  239.2 6.5 %all-reduce.1 = (f32[]{:T(128)}, f32[]{:T(128)}) all-reduce(f32[]{:T(128)} %get-tuple-element.9, f32[]{:T(128)} %reduce_sum.38), channel_id=1, replica_groups=mesh['wide'=8,'narrow'=4] {'narrow'}, use_global_device_ids=true, to_apply=%region_8.9 | all-reduce | flops 2 | bytes 16 | tf_op jit(solution)/shard_map/psum | solution.py:45
  247.8 1.3 fusion.7
  249.1 0.0 all-gather.5.cloned.1.call-update
  249.1 0.2 all-gather.7.cloned.1.call-start
  249.3 32.6 %all-gather.5.cloned.1.call-done = f32[1024,1024]{1,0:T(8,128)} async-done(((f32[256,1024]{1,0:T(8,128)}), f32[1024,1024]{1,0:T(8,128)}) %all-gather.5.cloned.1.call-update) | async-done | bytes 4194320 | tf_op jit(solution)/shard_map/all_gather | solution.py:50
  281.9 0.0 copy-start
  281.9 6.1 %fusion.10 = f32[256,1024]{1,0:T(8,128)S(1)} fusion(f32[1024,1024]{1,0:T(8,128)} %all-gather.5.cloned.1.call-done, f32[256,1024]{1,0:T(8,128)S(1)} %get-tuple-element.10, f32[]{:T(128)S(6)} %sqrt.6, f32[]{:T(128)S(6)} %add.43, s32[256]{0:T(256)S(1)} %iota_add_fusion), kind=kOutput, calls=%fused_computation.23 | convolution fusion | flops 3222274048 | bytes 6292488 | tf_op jit(solution)/shard_map/dot_general | solution.py:51
  288.1 0.0 copy-done
  288.1 3.7 %fusion.4 = f32[256,1024]{1,0:T(8,128)S(1)} fusion(f32[256,1024]{1,0:T(8,128)S(1)} %fusion.10, f32[1024,1024]{1,0:T(8,128)S(1)} %copy-done, s32[256]{0:T(256)S(1)} %iota_add_fusion), kind=kOutput, calls=%fused_computation.9 | convolution fusion | flops 3222274048 | bytes 6292480 | tf_op jit(solution)/shard_map/dot_general | solution.py:54
  291.9 0.0 copy-start.1
  291.9 4.7 %fusion.12 = f32[256,1024]{1,0:T(8,128)} fusion(f32[256,1024]{1,0:T(8,128)S(1)} %fusion.4, f32[1024,1024]{1,0:T(8,128)S(1)} %copy-done), kind=kOutput, calls=%fused_computation.25 | convolution fusion | flops 3221225472 | bytes 6291456 | tf_op jit(solution)/shard_map/dot_general | solution.py:58
  296.5 0.0 all-gather.7.cloned.1.call-update
  296.6 34.6 %all-gather.7.cloned.1.call-done = f32[1024,1024]{1,0:T(8,128)} async-done(((f32[256,1024]{1,0:T(8,128)}), f32[1024,1024]{1,0:T(8,128)}) %all-gather.7.cloned.1.call-update) | async-done | bytes 4194320 | tf_op jit(solution)/shard_map/all_gather | solution.py:64
  331.2 0.0 copy-done.1
  331.2 9.6 %divide_convert_fusion = bf16[512,1024]{1,0:T(8,128)(2,1)} fusion(f32[1024,1024]{1,0:T(8,128)} %all-gather.7.cloned.1.call-done, bf16[512,1024]{1,0:T(8,128)(2,1)S(1)} %copy-done.1, f32[]{:T(128)S(6)} %sqrt.7, f32[1024]{0:T(1024)S(1)} %get-tuple-element.12), kind=kOutput, calls=%fused_computation.2 | convolution fusion | flops 6444548096 | bytes 6295556 | tf_op jit(solution)/shard_map/dot_general | solution.py:62
  (4 shorter events, 0.0 us)
Async XLA Ops:
  6.5 97.0 %reduce-scatter.2.cloned.1.call-start = ((), (), s32[]{:S(2)}) async-start(), calls=%async_computation.1 | async-start | bytes 5242880 | tf_op jit(solution)/shard_map/reduce_scatter | solution.py:17
  58.7 171.4 %all-gather.9.cloned.1.call-start = ((), (), s32[]{:S(2)}) async-start(), calls=%async_computation.4 | async-start | bytes 9437184 | tf_op jit(solution)/shard_map/all_gather | solution.py:35
  103.6 178.4 %all-gather.5.cloned.1.call-start = ((), (), s32[]{:S(2)}) async-start(), calls=%async_computation.2 | async-start | bytes 5242880 | tf_op jit(solution)/shard_map/all_gather | solution.py:50
  249.1 82.1 %all-gather.7.cloned.1.call-start = ((), (), s32[]{:S(2)}) async-start(), calls=%async_computation.3 | async-start | bytes 5242880 | tf_op jit(solution)/shard_map/all_gather | solution.py:64
  281.9 6.1 %copy-start = (f32[1024,1024]{1,0:T(8,128)S(1)}, f32[1024,1024]{1,0:T(8,128)}, u32[]{:S(2)}) copy-start(f32[1024,1024]{1,0:T(8,128)} %all-gather.5.cloned.1.call-done) | copy-start | bytes 12582916
  291.9 39.3 %copy-start.1 = (bf16[512,1024]{1,0:T(8,128)(2,1)S(1)}, bf16[512,1024]{1,0:T(8,128)(2,1)}, u32[]{:S(2)}) copy-start(bf16[512,1024]{1,0:T(8,128)(2,1)} %param.2) | copy-start | bytes 3145732
Sparse Core Ops, SparseCore 0:
  58.9 44.6 reduce-scatter.1
  105.7 124.4 all-gather.8
  249.2 32.6 all-gather.4
  296.7 34.4 all-gather.6
